TPU v7x, 32 devices: a whole 2x2x4 slice. The times are simulated.
32 devices in a mesh: space: 8 (over z, x), vel: 4 (over y, core).
Axes of the slice: x: 2, y: 2, z: 4, core: 2. Of those that a mesh axis runs over, the one named last changes fastest.
Arguments:
- probe_field: float32 [2, 1024, 1024], P(None, 'space'), may hold values from -6 to 6
- control_field: float32 [2, 1024, 1024], P(None, 'space'), may hold values from -4 to 4
- optical_state: float32 [2, 64, 1024, 1024], P(None, 'vel', 'space'), may hold values from -3 to 3
- spin_state: float32 [2, 64, 1024, 1024], P(None, 'vel', 'space'), may hold values from -3 to 3
- doppler_shift: float32 [64], P('vel'), may hold values from -3 to 3
- class_weight: float32 [64], P('vel'), may hold values from 0.2 to 2
- gradient_shift: float32 [1024, 1024], P('space'), may hold values from -3 to 3
Outputs:
- probe_out: float32 [2, 1024, 1024], P(None, 'space')
- control_out: float32 [2, 1024, 1024], P(None, 'space')
- optical_out: float32 [2, 64, 1024, 1024], P(None, 'vel', 'space')
- spin_out: float32 [2, 64, 1024, 1024], P(None, 'vel', 'space')
All inputs are finite; a program needn't handle non-finite values.
Results may differ from a plain program's by a relative error of at most 0.000098.
Values sent between devices are 32-bit elements; how exact they have to be, the bound alone decides.
A program may use at most 192 MiB of HBM per device.

v0:
```python
import jax
import jax.numpy as jnp
import numpy as np
from jax import lax
from jax.sharding import PartitionSpec as P

GRID = 1024
VEL = 64
GAMMA = 1.0
DEPHASE = 0.1
DT = 0.25
COUPLE = 2.0
HIGHEST = lax.Precision.HIGHEST


def circulant_tables(grid_width):
    counter = np.arange(grid_width, dtype=np.int32)
    frequency = np.where(counter < grid_width // 2, counter, counter - grid_width)
    angles = (
        np.float32(np.pi)
        * (frequency * frequency % (2 * grid_width)).astype(np.float32)
        / np.float32(grid_width)
    )
    turns = counter[:, None] * counter[None, :] % grid_width
    argument = (
        np.float32(2.0 * np.pi) * turns.astype(np.float32) / np.float32(grid_width)
        - angles[None, :]
    )
    kernel_real = np.mean(np.cos(argument), axis=1)
    kernel_imag = np.mean(np.sin(argument), axis=1)
    offsets = (counter[:, None] - counter[None, :]) % grid_width
    return (kernel_real[offsets].astype(np.float32), kernel_imag[offsets].astype(np.float32))


def mix_left(table_real, table_imag, section):
    real_in, imag_in = (section[:, 0], section[:, 1])

    def product_of(table, values):
        return jnp.einsum("mn,fnk->fmk", table, values, precision=HIGHEST)

    return jnp.stack(
        [
            product_of(table_real, real_in) - product_of(table_imag, imag_in),
            product_of(table_real, imag_in) + product_of(table_imag, real_in),
        ],
        axis=1,
    )


def mix_right(section, table_real, table_imag):
    real_in, imag_in = (section[:, 0], section[:, 1])

    def product_of(values, table):
        return jnp.einsum("fmn,nk->fmk", values, table, precision=HIGHEST)

    return jnp.stack(
        [
            product_of(real_in, table_real) - product_of(imag_in, table_imag),
            product_of(imag_in, table_real) + product_of(real_in, table_imag),
        ],
        axis=1,
    )


def derivative(optical, spin_part, probe_part, control, doppler, gradient):
    optical_real, optical_imag = (optical[0], optical[1])
    spin_real, spin_imag = (spin_part[0], spin_part[1])
    probe_real, probe_imag = (probe_part[0], probe_part[1])
    control_real, control_imag = (control[0], control[1])
    rate_optical_real = (
        -GAMMA * optical_real
        + doppler * optical_imag
        - probe_imag
        - (control_real * spin_imag + control_imag * spin_real)
    )
    rate_optical_imag = (
        -GAMMA * optical_imag
        - doppler * optical_real
        + probe_real
        + (control_real * spin_real - control_imag * spin_imag)
    )
    rate_spin_real = (
        -DEPHASE * spin_real
        + gradient * spin_imag
        - (control_real * optical_imag - control_imag * optical_real)
    )
    rate_spin_imag = (
        -DEPHASE * spin_imag
        - gradient * spin_real
        + (control_real * optical_real + control_imag * optical_imag)
    )
    return (
        jnp.stack([rate_optical_real, rate_optical_imag]),
        jnp.stack([rate_spin_real, rate_spin_imag]),
    )


def midpoint(optical, spin_part, probe_part, control, doppler, gradient):
    rate_optical, rate_spin = derivative(optical, spin_part, probe_part, control, doppler, gradient)
    half_optical = optical + 0.5 * DT * rate_optical
    half_spin = spin_part + 0.5 * DT * rate_spin
    rate_optical, rate_spin = derivative(
        half_optical, half_spin, probe_part, control, doppler, gradient
    )
    return (optical + DT * rate_optical, spin_part + DT * rate_spin)


def add_source(complex_field, polarization):
    return jnp.stack(
        [complex_field[0] - COUPLE * polarization[1], complex_field[1] + COUPLE * polarization[0]]
    )


def shards(
    probe_field,
    control_field,
    optical_state,
    spin_state,
    doppler_shift,
    class_weight,
    gradient_shift,
):
    grid_width = GRID
    quarter_width = grid_width // lax.axis_size("vel")
    table_real, table_imag = circulant_tables(grid_width)
    full_real = jnp.asarray(table_real)
    full_imag = jnp.asarray(table_imag)

    def row_mix(section):
        blended = mix_left(
            full_real,
            full_imag,
            lax.all_to_all(section, "space", split_axis=3, concat_axis=2, tiled=True),
        )
        return lax.all_to_all(blended, "space", split_axis=2, concat_axis=3, tiled=True)

    def spread(section):
        return lax.all_gather(section, "vel", axis=3, tiled=True)

    stacked = jnp.stack([probe_field, control_field])
    col_start = lax.axis_index("vel") * quarter_width
    quart_real = lax.dynamic_slice_in_dim(full_real, col_start, quarter_width, 1)
    quart_imag = lax.dynamic_slice_in_dim(full_imag, col_start, quarter_width, 1)
    stacked = spread(row_mix(mix_right(stacked, quart_real, quart_imag)))
    optical_new, spin_new = midpoint(
        optical_state,
        spin_state,
        stacked[0],
        stacked[1],
        doppler_shift[:, None, None],
        gradient_shift,
    )
    weighted = jnp.einsum("cvrn,v->crn", optical_new, class_weight, precision=HIGHEST) / VEL
    polarization = lax.psum_scatter(weighted, "vel", scatter_dimension=2, tiled=True)
    probe_part = lax.dynamic_slice_in_dim(stacked[0], col_start, quarter_width, 2)
    control_part = lax.dynamic_slice_in_dim(stacked[1], col_start, quarter_width, 2)
    section = jnp.stack([add_source(probe_part, polarization), control_part])
    stacked = mix_right(spread(row_mix(section)), full_real, full_imag)
    return (stacked[0], stacked[1], optical_new, spin_new)


def solution(mesh):
    return jax.shard_map(
        shards,
        mesh=mesh,
        in_specs=(
            P(None, "space", None),
            P(None, "space", None),
            P(None, "vel", "space", None),
            P(None, "vel", "space", None),
            P("vel"),
            P("vel"),
            P("space", None),
        ),
        out_specs=(
            P(None, "space", None),
            P(None, "space", None),
            P(None, "vel", "space", None),
            P(None, "vel", "space", None),
        ),
        check_vma=False,
    )
```

profile of v0, /device:TPU:0, one launch (start us, length us, event | category | flops | bytes accessed | tf_op | source)
XLA Modules:
  0.0 411.2 jit_solution(229504936186904210)
XLA Ops:
  17.8 21.6 %all_to_all.72 = f32[2,2,128,256]{2,0,1,3:T(2,128)S(1)} all-to-all(f32[2,2,128,256]{2,0,1,3:T(2,128)S(1)} %copy.38), channel_id=1, replica_groups=mesh['space'=8,'vel'=4] {'space'}, dimensions={3} | all-to-all | bytes 1048576 | tf_op jit(solution)/shard_map/all_to_all | solution.py:133
  39.9 6.4 %fusion.35 = f32[2,32,1024]{2,1,0:T(8,128)S(1)} fusion(f32[1024,1024,1]{1,0,2:T(8,128)} %constant.31, f32[2,2,1024,32]{2,3,0,1:T(8,128)S(1)} %all_to_all.55), kind=kOutput, calls=%fused_computation.75 | convolution fusion | flops 805306368 | bytes 4718592 | tf_op jit(solution)/shard_map/mn,fnk->fmk/dot_general | solution.py:39
  46.3 6.3 %fusion.34 = f32[2,32,1024]{2,1,0:T(8,128)S(1)} fusion(f32[1024,1024,1]{1,0,2:T(8,128)} %constant.31, f32[2,2,1024,32]{2,3,0,1:T(8,128)S(1)} %all_to_all.55), kind=kOutput, calls=%fused_computation.74 | convolution fusion | flops 805306368 | bytes 4718592 | tf_op jit(solution)/shard_map/mn,fnk->fmk/dot_general | solution.py:39
  52.5 4.1 %fusion.10 = f32[2,1,1024,32]{2,3,0,1:T(8,128)S(1)} fusion(f32[2,32,1024]{2,1,0:T(8,128)S(1)} %fusion.35, f32[1024,1024,1]{1,0,2:T(8,128)S(1)} %copy-done.1, f32[2,2,1024,32]{2,3,0,1:T(8,128)S(1)} %all_to_all.55), kind=kOutput, calls=%fused_computation.31 | convolution fusion | flops 805371904 | bytes 4980736 | tf_op jit(solution)/shard_map/mn,fnk->fmk/dot_general | solution.py:39
  56.6 4.6 %fusion.11 = f32[2,1,1024,32]{2,3,0,1:T(8,128)S(1)} fusion(f32[2,32,1024]{2,1,0:T(8,128)S(1)} %fusion.34, f32[1024,1024,1]{1,0,2:T(8,128)S(1)} %copy-done.1, f32[2,2,1024,32]{2,3,0,1:T(8,128)S(1)} %all_to_all.55), kind=kOutput, calls=%fused_computation.33 | convolution fusion | flops 805371904 | bytes 4980736 | tf_op jit(solution)/shard_map/mn,fnk->fmk/dot_general | solution.py:39
  64.8 17.7 %all_to_all.73 = f32[8,1,16384]{2,1,0:T(1,128)S(1)} all-to-all(f32[8,1,16384]{2,1,0:T(1,128)S(1)} %reshape.33), channel_id=1, replica_groups=mesh['space'=8,'vel'=4] {'space'}, dimensions={0} | all-to-all | bytes 1048576 | tf_op jit(solution)/shard_map/all_to_all | solution.py:135
  89.3 21.7 %all-gather.3.cloned.1.call-done = f32[2,2,128,1024]{2,3,1,0:T(8,128)} async-done(((f32[2,2,128,256]{2,3,1,0:T(8,128)}), f32[2,2,128,1024]{2,3,1,0:T(8,128)}) %all-gather.3.cloned.1.call-update) | async-done | bytes 2097168 | tf_op jit(solution)/shard_map/all_gather | solution.py:138
  113.5 18.6 %subtract_subtract_fusion.1 = (f32[1,16,128,1024]{3,2,1,0:T(8,128)}, f32[1,16,128,1024]{3,2,1,0:T(8,128)}) fusion(f32[2,16,128,1024]{3,2,1,0:T(8,128)} %param.12, f32[2,16,128,1024]{3,2,1,0:T(8,128)} %param.11, f32[128,1024]{1,0:T(8,128)S(1)} %copy-done.9, f32[128,1024]{1,0:T(8,128)S(1)} %copy.46, f32[128,1024]{1,0:T(8,128)S(1)} %copy.45), kind=kLoop, calls=%fused_computation.15 | loop fusion | flops 29360128 | bytes 51904512 | tf_op jit(solution)/shard_map/sub | solution.py:83
  132.1 18.4 %add_subtract_fusion.1 = (f32[1,16,128,1024]{3,2,1,0:T(8,128)}, f32[1,16,128,1024]{3,2,1,0:T(8,128)}) fusion(f32[2,16,128,1024]{3,2,1,0:T(8,128)} %param.12, f32[2,16,128,1024]{3,2,1,0:T(8,128)} %param.11, f32[128,1024]{1,0:T(8,128)S(1)} %copy.46, f32[128,1024]{1,0:T(8,128)S(1)} %copy.45, f32[128,1024]{1,0:T(8,128)S(1)} %copy.44, f32[16]{0:T(128)S(1)} %copy-done.10, ...), kind=kLoop, calls=%fused_computation.17 | loop fusion | flops 33554432 | bytes 52428864 | tf_op jit(solution)/shard_map/sub | solution.py:71
  150.5 33.9 %fusion = (f32[2,16,128,1024]{3,2,1,0:T(8,128)}, f32[2,16,128,1024]{3,2,1,0:T(8,128)}) fusion(f32[2,16,128,1024]{3,2,1,0:T(8,128)} %param.11, f32[1,16,128,1024]{3,2,1,0:T(8,128)} %get-tuple-element.11, f32[1,16,128,1024]{3,2,1,0:T(8,128)} %get-tuple-element.10, f32[2,16,128,1024]{3,2,1,0:T(8,128)} %param.12, f32[1,16,128,1024]{3,2,1,0:T(8,128)} %get-tuple-element.7, ...), kind=kLoop, calls=%fused_computation.1 | loop fusion | flops 25165824 | bytes 100663296 | tf_op jit(solution)/shard_map/add | solution.py:100
  184.4 18.4 %add_subtract_fusion = (f32[1,16,128,1024]{3,2,1,0:T(8,128)}, f32[1,16,128,1024]{3,2,1,0:T(8,128)}) fusion(f32[2,16,128,1024]{3,2,1,0:T(8,128)} %get-tuple-element.23, f32[2,16,128,1024]{3,2,1,0:T(8,128)} %get-tuple-element.22, f32[128,1024]{1,0:T(8,128)S(1)} %copy.46, f32[128,1024]{1,0:T(8,128)S(1)} %copy.45, f32[128,1024]{1,0:T(8,128)S(1)} %copy.44, ...), kind=kLoop, calls=%fused_computation.13 | loop fusion | flops 33554432 | bytes 52428864 | tf_op jit(solution)/shard_map/sub | solution.py:71
  202.7 11.9 %fusion.2 = f32[2,16,128,1024]{3,2,1,0:T(8,128)S(1)} fusion(f32[2,16,128,1024]{3,2,1,0:T(8,128)} %param.11, f32[1,16,128,1024]{3,2,1,0:T(8,128)} %get-tuple-element.9, f32[1,16,128,1024]{3,2,1,0:T(8,128)} %get-tuple-element.8), kind=kLoop, calls=%fused_computation.5 | loop fusion | flops 12582912 | bytes 50331648 | tf_op jit(solution)/shard_map/add | solution.py:105
  214.6 6.2 %copy-done.4 = f32[2,16,128,1024]{3,2,1,0:T(8,128)} copy-done((f32[2,16,128,1024]{3,2,1,0:T(8,128)}, f32[2,16,128,1024]{3,2,1,0:T(8,128)S(1)}, u32[]{:S(2)}) %copy-start.4) | copy-done | bytes 16777240
  220.8 16.7 %fusion.4 = f32[1,2,128,1024]{3,0,2,1:T(1,128)} fusion(f32[2,16,128,1024]{3,2,1,0:T(8,128)S(1)} %fusion.2, f32[16]{0:T(128)S(1)} %copy-done), kind=kOutput, calls=%fused_computation.8 | convolution fusion | flops 50331648 | bytes 17825856 | tf_op jit(solution)/shard_map/cvrn,v->crn/dot_general | solution.py:153
  244.6 23.8 %reduce-scatter.2.cloned.1.call-done = f32[2,128,256]{1,2,0:T(8,128)} async-done(((f32[2,128,1024]{1,2,0:T(8,128)}), f32[2,128,256]{1,2,0:T(8,128)}) %reduce-scatter.2.cloned.1.call-update) | async-done | bytes 262160 | tf_op jit(solution)/shard_map/reduce_scatter | solution.py:154
  270.0 19.7 %all_to_all.74 = f32[2,2,128,256]{2,1,0,3:T(2,128)S(1)} all-to-all(f32[2,2,128,256]{2,1,0,3:T(2,128)S(1)} %copy.48), channel_id=1, replica_groups=mesh['space'=8,'vel'=4] {'space'}, dimensions={3} | all-to-all | bytes 1048576 | tf_op jit(solution)/shard_map/all_to_all | solution.py:133
  290.1 6.4 %fusion.37 = f32[2,32,1024]{2,1,0:T(8,128)S(1)} fusion(f32[1024,1024,1]{1,0,2:T(8,128)} %constant.31, f32[2,2,1024,32]{2,3,0,1:T(8,128)S(1)} %all_to_all.63), kind=kOutput, calls=%fused_computation.77 | convolution fusion | flops 805306368 | bytes 4718592 | tf_op jit(solution)/shard_map/mn,fnk->fmk/dot_general | solution.py:39
  296.5 6.3 %fusion.36 = f32[2,32,1024]{2,1,0:T(8,128)S(1)} fusion(f32[1024,1024,1]{1,0,2:T(8,128)} %constant.31, f32[2,2,1024,32]{2,3,0,1:T(8,128)S(1)} %all_to_all.63), kind=kOutput, calls=%fused_computation.76 | convolution fusion | flops 805306368 | bytes 4718592 | tf_op jit(solution)/shard_map/mn,fnk->fmk/dot_general | solution.py:39
  306.9 4.3 %fusion.9 = f32[2,1,1024,32]{2,3,0,1:T(8,128)S(1)} fusion(f32[2,32,1024]{2,1,0:T(8,128)S(1)} %fusion.36, f32[1024,1024,1]{1,0,2:T(8,128)S(1)} %copy-done.2, f32[2,2,1024,32]{2,3,0,1:T(8,128)S(1)} %all_to_all.63), kind=kOutput, calls=%fused_computation.29 | convolution fusion | flops 805371904 | bytes 4980736 | tf_op jit(solution)/shard_map/mn,fnk->fmk/dot_general | solution.py:39
  317.7 17.7 %all_to_all.75 = f32[8,1,16384]{2,1,0:T(1,128)S(1)} all-to-all(f32[8,1,16384]{2,1,0:T(1,128)} %reshape.35), channel_id=1, replica_groups=mesh['space'=8,'vel'=4] {'space'}, dimensions={0} | all-to-all | bytes 1048576 | tf_op jit(solution)/shard_map/all_to_all | solution.py:135
  345.5 20.3 %subtract_subtract_fusion = (f32[1,16,128,1024]{3,2,1,0:T(8,128)}, f32[1,16,128,1024]{3,2,1,0:T(8,128)}) fusion(f32[2,16,128,1024]{3,2,1,0:T(8,128)} %get-tuple-element.23, f32[2,16,128,1024]{3,2,1,0:T(8,128)} %get-tuple-element.22, f32[128,1024]{1,0:T(8,128)} %param.15, f32[128,1024]{1,0:T(8,128)S(1)} %copy.46, f32[128,1024]{1,0:T(8,128)S(1)} %copy.45), kind=kLoop, calls=%fused_computation.11 | loop fusion | flops 29360128 | bytes 51904512 | tf_op jit(solution)/shard_map/sub | solution.py:83
  365.8 17.2 %fusion.3 = f32[2,16,128,1024]{3,2,1,0:T(8,128)} fusion(f32[2,16,128,1024]{3,2,1,0:T(8,128)} %param.12, f32[1,16,128,1024]{3,2,1,0:T(8,128)} %get-tuple-element.5, f32[1,16,128,1024]{3,2,1,0:T(8,128)} %get-tuple-element.4), kind=kLoop, calls=%fused_computation.7 | loop fusion | flops 12582912 | bytes 50331648 | tf_op jit(solution)/shard_map/add | solution.py:105
  383.1 6.2 %fusion.31 = f32[2,128,1024]{2,1,0:T(8,128)S(1)} fusion(f32[1024,1024,1]{1,0,2:T(8,128)} %constant.31, f32[2,2,128,1024]{3,2,0,1:T(8,128)} %all-gather.5.cloned.1.call-done), kind=kOutput, calls=%fused_computation.60 | convolution fusion | flops 3221225472 | bytes 6291456 | tf_op jit(solution)/shard_map/fmn,nk->fmk/dot_general | solution.py:54
  389.2 6.2 %fusion.30 = f32[2,128,1024]{2,1,0:T(8,128)S(1)} fusion(f32[1024,1024,1]{1,0,2:T(8,128)} %constant.31, f32[2,2,128,1024]{3,2,0,1:T(8,128)} %all-gather.5.cloned.1.call-done), kind=kOutput, calls=%fused_computation.59 | convolution fusion | flops 3221225472 | bytes 6291456 | tf_op jit(solution)/shard_map/fmn,nk->fmk/dot_general | solution.py:54
  (71 shorter events, 62.4 us)
Async XLA Ops:
  7.2 213.6 %copy-start = (f32[16]{0:T(128)S(1)}, f32[16]{0:T(128)}, u32[]{:S(2)}) copy-start(f32[16]{0:T(128)} %param.14) | copy-start | bytes 196
  7.2 7.9 %copy-start.5 = (f32[2,128,1024]{2,1,0:T(8,128)S(1)}, f32[2,128,1024]{2,1,0:T(8,128)}, u32[]{:S(2)}) copy-start(f32[2,128,1024]{2,1,0:T(8,128)} %param.10) | copy-start | bytes 3145732
  7.2 7.9 %copy-start.6 = (f32[2,128,1024]{2,1,0:T(8,128)S(1)}, f32[2,128,1024]{2,1,0:T(8,128)}, u32[]{:S(2)}) copy-start(f32[2,128,1024]{2,1,0:T(8,128)} %param.9) | copy-start | bytes 3145732
  7.2 103.8 %all-gather.3.cloned.1.call-start = ((), (), s32[]{:S(2)}) async-start(), calls=%async_computation.5 | async-start | bytes 2621440 | tf_op jit(solution)/shard_map/all_gather | solution.py:138
  39.8 12.7 %copy-start.1 = (f32[1024,1024,1]{1,0,2:T(8,128)S(1)}, f32[1024,1024,1]{1,0,2:T(8,128)}, u32[]{:S(2)}) copy-start(f32[1024,1024,1]{1,0,2:T(8,128)} %constant.32) | copy-start | bytes 12582916
  64.8 48.7 %copy-start.9 = (f32[128,1024]{1,0:T(8,128)S(1)}, f32[128,1024]{1,0:T(8,128)}, u32[]{:S(2)}) copy-start(f32[128,1024]{1,0:T(8,128)} %param.15) | copy-start | bytes 1572868
  89.2 179.1 %reduce-scatter.2.cloned.1.call-start = ((), (), s32[]{:S(2)}) async-start(), calls=%async_computation.6 | async-start | bytes 1310720 | tf_op jit(solution)/shard_map/reduce_scatter | solution.py:154
  113.5 18.6 %copy-start.10 = (f32[16]{0:T(128)S(1)}, f32[16]{0:T(128)}, u32[]{:S(2)}) copy-start(f32[16]{0:T(128)} %param.13) | copy-start | bytes 196
  214.6 6.2 %copy-start.4 = (f32[2,16,128,1024]{3,2,1,0:T(8,128)}, f32[2,16,128,1024]{3,2,1,0:T(8,128)S(1)}, u32[]{:S(2)}) copy-start(f32[2,16,128,1024]{3,2,1,0:T(8,128)S(1)} %fusion.2) | copy-start | bytes 50331652
  220.8 22.7 %copy-start.7 = (f32[2,2,128,1024]{2,3,1,0:T(8,128)S(1)}, f32[2,2,128,1024]{2,3,1,0:T(8,128)}, u32[]{:S(2)}) copy-start(f32[2,2,128,1024]{2,3,1,0:T(8,128)} %all-gather.3.cloned.1.call-done) | copy-start | bytes 6291460
  243.4 139.7 %all-gather.5.cloned.1.call-start = ((), (), s32[]{:S(2)}) async-start(), calls=%async_computation.7 | async-start | bytes 2621440 | tf_op jit(solution)/shard_map/all_gather | solution.py:138
  290.1 12.7 %copy-start.2 = (f32[1024,1024,1]{1,0,2:T(8,128)S(1)}, f32[1024,1024,1]{1,0,2:T(8,128)}, u32[]{:S(2)}) copy-start(f32[1024,1024,1]{1,0,2:T(8,128)} %constant.32) | copy-start | bytes 12582916
  383.1 12.4 %copy-start.3 = (f32[1024,1024,1]{1,0,2:T(8,128)S(1)}, f32[1024,1024,1]{1,0,2:T(8,128)}, u32[]{:S(2)}) copy-start(f32[1024,1024,1]{1,0,2:T(8,128)} %constant.32) | copy-start | bytes 12582916
  383.1 12.4 %copy-start.8 = (f32[2,2,128,1024]{3,2,0,1:T(8,128)S(1)}, f32[2,2,128,1024]{3,2,0,1:T(8,128)}, u32[]{:S(2)}) copy-start(f32[2,2,128,1024]{3,2,0,1:T(8,128)} %all-gather.5.cloned.1.call-done) | copy-start | bytes 6291460
Sparse Core Ops, SparseCore 0:
  89.3 21.6 all-gather.2
  243.5 24.8 reduce-scatter.1
  345.7 20.6 all-gather.4
where the time goes:
time: 416 us; the launch traced here: 411 us
  other arithmetic  149 us (36%)
  matrix products  89.2 us (21%)
  blocking collectives  76.7 us (18%)
  waiting for transfers between devices  45.6 us (11%)
  local copies, waits for them, and re-layouts  36 us (9%)
  between operations  14.3 us (3%)
    dot_general x8, matrix products, product_of(): return jnp.einsum('mn,fnk->fmk', table, values, precision=HIGHEST)  42.5 us
    all_to_all x2, blocking collectives, row_mix(): lax.all_to_all(section, 'space', split_axis=3, concat_axis=2, tiled=True)  41.3 us
    sub x2, other arithmetic, derivative(): -DEPHASE * spin_real + gradient * spin_imag  38.9 us
    sub x2, other arithmetic, derivative(): -GAMMA * optical_real + doppler * optical_imag - probe_imag  36.8 us
    all_to_all x2, blocking collectives, row_mix(): lax.all_to_all(blended, 'space', split_axis=2, concat_axis=3, tiled=True)  35.4 us
    add x1, other arithmetic, midpoint(): half_optical = optical + 0.5 * DT * rate_optical  33.9 us
    dot_general x8, matrix products, product_of(): return jnp.einsum('fmn,nk->fmk', values, table, precision=HIGHEST)  30 us
    add x2, other arithmetic, midpoint(): return (optical + DT * rate_optical, spin_part + DT * rate_spin)  29.1 us
  transfers between devices with their start and end apart: 3, of which 2 were waited for; matrix products, arithmetic and copies ran while one was open for 9% of the time, Pallas kernels for 0%

commit v1 on v0

--- a/solution.py
+++ b/solution.py
@@ -132,7 +132,19 @@
             full_imag,
             lax.all_to_all(section, "space", split_axis=3, concat_axis=2, tiled=True),
         )
-        return lax.all_to_all(blended, "space", split_axis=2, concat_axis=3, tiled=True)
+
+        def handle_rings_now(on_dim, net_axis, d_out, original):
+            return jnp.concatenate(
+                lax.all_to_all(
+                    jnp.stack(jnp.split(original, lax.axis_size(net_axis), axis=on_dim), axis=0),
+                    net_axis,
+                    0,
+                    0,
+                ),
+                axis=d_out,
+            )
+
+        return handle_rings_now(2, net_axis="space", d_out=3, original=blended)
 
     def spread(section):
         return lax.all_gather(section, "vel", axis=3, tiled=True)

time: 416 us -> 399 us (0.959)
  local copies, waits for them, and re-layouts: 36 us -> 16.8 us
  matrix products: 89.2 us -> 97.7 us
  other arithmetic: 149 us -> 143 us
    unnamed x26 -> x24, local copies, waits for them, and re-layouts: 15.7 us -> 6.22 us
    dot_general x8, matrix products: 42.5 us -> 51 us  [product_of(): return jnp.einsum('mn,fnk->fmk', table, values, precision=HIGHEST)]
    all_to_all x4 -> x0, local copies, waits for them, and re-layouts: 7.43 us -> none  [row_mix(): lax.all_to_all(blended, 'space', split_axis=2, concat_axis=3, tiled=True)]
    all_to_all x2 -> x0, other arithmetic: 4.84 us -> none  [row_mix(): lax.all_to_all(blended, 'space', split_axis=2, concat_axis=3, tiled=True)]
    another operation x2 -> x0, local copies, waits for them, and re-layouts: 4.17 us -> none  [mix_left(): jnp.stack([product_of(table_real, real_in) - product_of(table_imag, imag_...]
  transfers between devices with their start and end apart: 3 -> 3, of which waited for: 2 -> 2; matrix products, arithmetic and copies ran while one was open for 9% -> 10% of each run, Pallas kernels for 0% -> 0%
where the time goes in v1:
time: 399 us; the launch traced here: 394 us
  other arithmetic  143 us (36%)
  matrix products  97.7 us (24%)
  blocking collectives  76.3 us (19%)
  waiting for transfers between devices  45.6 us (11%)
  local copies, waits for them, and re-layouts  16.8 us (4%)
  between operations  14.4 us (4%)
    dot_general x8, matrix products, product_of(): return jnp.einsum('mn,fnk->fmk', table, values, precision=HIGHEST)  51 us
    all_to_all x2, blocking collectives, row_mix(): lax.all_to_all(section, 'space', split_axis=3, concat_axis=2, tiled=True)  41.3 us
    sub x2, other arithmetic, derivative(): -DEPHASE * spin_real + gradient * spin_imag  38.4 us
    sub x2, other arithmetic, derivative(): -GAMMA * optical_real + doppler * optical_imag - probe_imag  36.7 us
    all_to_all x2, blocking collectives, handle_rings_now(): lax.all_to_all(jnp.stack(jnp.split(original, lax.axis_size(net_axis), axi...  35.1 us
    add x1, other arithmetic, midpoint(): half_optical = optical + 0.5 * DT * rate_optical  33.9 us
    dot_general x8, matrix products, product_of(): return jnp.einsum('fmn,nk->fmk', values, table, precision=HIGHEST)  30 us
    add x2, other arithmetic, midpoint(): return (optical + DT * rate_optical, spin_part + DT * rate_spin)  29.1 us
  transfers between devices with their start and end apart: 3, of which 2 were waited for; matrix products, arithmetic and copies ran while one was open for 10% of the time, Pallas kernels for 0%

profile of v1, /device:TPU:0, one launch (start us, length us, event | category | flops | bytes accessed | tf_op | source)
XLA Modules:
  0.0 394.2 jit_solution(4723277360425857515)
XLA Ops:
  17.8 21.6 %all_to_all.46 = f32[2,2,128,256]{2,0,1,3:T(2,128)S(1)} all-to-all(f32[2,2,128,256]{2,0,1,3:T(2,128)S(1)} %copy.24), channel_id=1, replica_groups=mesh['space'=8,'vel'=4] {'space'}, dimensions={3} | all-to-all | bytes 1048576 | tf_op jit(solution)/shard_map/all_to_all | solution.py:133
  39.9 6.4 %fusion.34 = f32[2,32,1024]{2,1,0:T(8,128)S(1)} fusion(f32[1024,1024,1]{1,0,2:T(8,128)} %constant.31, f32[2,2,1024,32]{2,3,0,1:T(8,128)S(1)} %all_to_all.35), kind=kOutput, calls=%fused_computation.100 | convolution fusion | flops 805306368 | bytes 4718592 | tf_op jit(solution)/shard_map/mn,fnk->fmk/dot_general | solution.py:39
  46.3 6.3 %fusion.35 = f32[2,32,1024]{2,1,0:T(8,128)S(1)} fusion(f32[1024,1024,1]{1,0,2:T(8,128)} %constant.31, f32[2,2,1024,32]{2,3,0,1:T(8,128)S(1)} %all_to_all.35), kind=kOutput, calls=%fused_computation.101 | convolution fusion | flops 805306368 | bytes 4718592 | tf_op jit(solution)/shard_map/mn,fnk->fmk/dot_general | solution.py:39
  52.5 4.1 %fusion.11 = f32[2,1,1024,32]{2,3,0,1:T(8,128)S(1)} fusion(f32[2,32,1024]{2,1,0:T(8,128)S(1)} %fusion.34, f32[1024,1024,1]{1,0,2:T(8,128)S(1)} %copy-done.1, f32[2,2,1024,32]{2,3,0,1:T(8,128)S(1)} %all_to_all.35), kind=kOutput, calls=%fused_computation.33 | convolution fusion | flops 805371904 | bytes 4980736 | tf_op jit(solution)/shard_map/mn,fnk->fmk/dot_general | solution.py:39
  56.6 13.2 %fusion.10 = f32[2,1,1024,32]{2,3,0,1:T(8,128)S(1)} fusion(f32[2,32,1024]{2,1,0:T(8,128)S(1)} %fusion.35, f32[1024,1024,1]{1,0,2:T(8,128)S(1)} %copy-done.1, f32[2,2,1024,32]{2,3,0,1:T(8,128)S(1)} %all_to_all.35), kind=kOutput, calls=%fused_computation.31 | convolution fusion | flops 805371904 | bytes 4980736 | tf_op jit(solution)/shard_map/mn,fnk->fmk/dot_general | solution.py:39
  70.0 17.5 %all_to_all.47 = f32[8,2,2,128,32]{3,4,1,2,0:T(8,128)S(1)} all-to-all(f32[8,2,2,128,32]{3,4,1,2,0:T(8,128)S(1)} %fusion.87), channel_id=1, replica_groups=mesh['space'=8,'vel'=4] {'space'}, dimensions={0} | all-to-all | bytes 1048576 | tf_op jit(solution)/shard_map/all_to_all | solution.py:138
  88.4 21.7 %all-gather.3.cloned.1.call-done = f32[2,2,128,1024]{2,3,1,0:T(8,128)} async-done(((f32[2,2,128,256]{2,3,1,0:T(8,128)}), f32[2,2,128,1024]{2,3,1,0:T(8,128)}) %all-gather.3.cloned.1.call-update) | async-done | bytes 2097168 | tf_op jit(solution)/shard_map/all_gather | solution.py:150
  112.7 18.4 %subtract_subtract_fusion.1 = (f32[1,16,128,1024]{3,2,1,0:T(8,128)}, f32[1,16,128,1024]{3,2,1,0:T(8,128)}) fusion(f32[2,16,128,1024]{3,2,1,0:T(8,128)} %param.12, f32[2,16,128,1024]{3,2,1,0:T(8,128)} %param.11, f32[128,1024]{1,0:T(8,128)S(1)} %copy-done.9, f32[128,1024]{1,0:T(8,128)S(1)} %copy.30, f32[128,1024]{1,0:T(8,128)S(1)} %copy.29), kind=kLoop, calls=%fused_computation.15 | loop fusion | flops 29360128 | bytes 51904512 | tf_op jit(solution)/shard_map/sub | solution.py:83
  131.1 18.4 %add_subtract_fusion.1 = (f32[1,16,128,1024]{3,2,1,0:T(8,128)}, f32[1,16,128,1024]{3,2,1,0:T(8,128)}) fusion(f32[2,16,128,1024]{3,2,1,0:T(8,128)} %param.12, f32[2,16,128,1024]{3,2,1,0:T(8,128)} %param.11, f32[128,1024]{1,0:T(8,128)S(1)} %copy.30, f32[128,1024]{1,0:T(8,128)S(1)} %copy.29, f32[128,1024]{1,0:T(8,128)S(1)} %copy.28, f32[16]{0:T(128)S(1)} %copy-done.11, ...), kind=kLoop, calls=%fused_computation.17 | loop fusion | flops 33554432 | bytes 52428864 | tf_op jit(solution)/shard_map/sub | solution.py:71
  149.4 33.9 %fusion = (f32[2,16,128,1024]{3,2,1,0:T(8,128)}, f32[2,16,128,1024]{3,2,1,0:T(8,128)}) fusion(f32[2,16,128,1024]{3,2,1,0:T(8,128)} %param.11, f32[1,16,128,1024]{3,2,1,0:T(8,128)} %get-tuple-element.11, f32[1,16,128,1024]{3,2,1,0:T(8,128)} %get-tuple-element.10, f32[2,16,128,1024]{3,2,1,0:T(8,128)} %param.12, f32[1,16,128,1024]{3,2,1,0:T(8,128)} %get-tuple-element.7, ...), kind=kLoop, calls=%fused_computation.1 | loop fusion | flops 25165824 | bytes 100663296 | tf_op jit(solution)/shard_map/add | solution.py:100
  183.3 18.4 %add_subtract_fusion = (f32[1,16,128,1024]{3,2,1,0:T(8,128)}, f32[1,16,128,1024]{3,2,1,0:T(8,128)}) fusion(f32[2,16,128,1024]{3,2,1,0:T(8,128)} %get-tuple-element.23, f32[2,16,128,1024]{3,2,1,0:T(8,128)} %get-tuple-element.22, f32[128,1024]{1,0:T(8,128)S(1)} %copy.30, f32[128,1024]{1,0:T(8,128)S(1)} %copy.29, f32[128,1024]{1,0:T(8,128)S(1)} %copy.28, ...), kind=kLoop, calls=%fused_computation.13 | loop fusion | flops 33554432 | bytes 52428864 | tf_op jit(solution)/shard_map/sub | solution.py:71
  201.7 11.9 %fusion.2 = f32[2,16,128,1024]{3,2,1,0:T(8,128)S(1)} fusion(f32[2,16,128,1024]{3,2,1,0:T(8,128)} %param.11, f32[1,16,128,1024]{3,2,1,0:T(8,128)} %get-tuple-element.9, f32[1,16,128,1024]{3,2,1,0:T(8,128)} %get-tuple-element.8), kind=kLoop, calls=%fused_computation.5 | loop fusion | flops 12582912 | bytes 50331648 | tf_op jit(solution)/shard_map/add | solution.py:105
  213.6 6.2 %copy-done.4 = f32[2,16,128,1024]{3,2,1,0:T(8,128)} copy-done((f32[2,16,128,1024]{3,2,1,0:T(8,128)}, f32[2,16,128,1024]{3,2,1,0:T(8,128)S(1)}, u32[]{:S(2)}) %copy-start.4) | copy-done | bytes 16777240
  219.7 16.7 %fusion.4 = f32[1,2,128,1024]{3,0,2,1:T(1,128)} fusion(f32[2,16,128,1024]{3,2,1,0:T(8,128)S(1)} %fusion.2, f32[16]{0:T(128)S(1)} %copy-done), kind=kOutput, calls=%fused_computation.8 | convolution fusion | flops 50331648 | bytes 17825856 | tf_op jit(solution)/shard_map/cvrn,v->crn/dot_general | solution.py:165
  243.5 23.8 %reduce-scatter.2.cloned.1.call-done = f32[2,128,256]{1,2,0:T(8,128)} async-done(((f32[2,128,1024]{1,2,0:T(8,128)}), f32[2,128,256]{1,2,0:T(8,128)}) %reduce-scatter.2.cloned.1.call-update) | async-done | bytes 262160 | tf_op jit(solution)/shard_map/reduce_scatter | solution.py:166
  268.9 19.7 %all_to_all.48 = f32[2,2,128,256]{2,1,0,3:T(2,128)S(1)} all-to-all(f32[2,2,128,256]{2,1,0,3:T(2,128)S(1)} %copy.32), channel_id=1, replica_groups=mesh['space'=8,'vel'=4] {'space'}, dimensions={3} | all-to-all | bytes 1048576 | tf_op jit(solution)/shard_map/all_to_all | solution.py:133
  289.1 6.4 %fusion.36 = f32[2,32,1024]{2,1,0:T(8,128)S(1)} fusion(f32[1024,1024,1]{1,0,2:T(8,128)} %constant.31, f32[2,2,1024,32]{2,3,0,1:T(8,128)S(1)} %all_to_all.40), kind=kOutput, calls=%fused_computation.102 | convolution fusion | flops 805306368 | bytes 4718592 | tf_op jit(solution)/shard_map/mn,fnk->fmk/dot_general | solution.py:39
  295.5 6.3 %fusion.37 = f32[2,32,1024]{2,1,0:T(8,128)S(1)} fusion(f32[1024,1024,1]{1,0,2:T(8,128)} %constant.31, f32[2,2,1024,32]{2,3,0,1:T(8,128)S(1)} %all_to_all.40), kind=kOutput, calls=%fused_computation.103 | convolution fusion | flops 805306368 | bytes 4718592 | tf_op jit(solution)/shard_map/mn,fnk->fmk/dot_general | solution.py:39
  305.8 4.3 %fusion.8 = f32[2,1,1024,32]{2,3,0,1:T(8,128)S(1)} fusion(f32[2,32,1024]{2,1,0:T(8,128)S(1)} %fusion.37, f32[1024,1024,1]{1,0,2:T(8,128)S(1)} %copy-done.2, f32[2,2,1024,32]{2,3,0,1:T(8,128)S(1)} %all_to_all.40), kind=kOutput, calls=%fused_computation.27 | convolution fusion | flops 805371904 | bytes 4980736 | tf_op jit(solution)/shard_map/mn,fnk->fmk/dot_general | solution.py:39
  310.3 17.5 %all_to_all.49 = f32[8,2,2,128,32]{3,4,1,2,0:T(8,128)S(1)} all-to-all(f32[8,2,2,128,32]{3,4,1,2,0:T(8,128)S(1)} %fusion.85), channel_id=1, replica_groups=mesh['space'=8,'vel'=4] {'space'}, dimensions={0} | all-to-all | bytes 1048576 | tf_op jit(solution)/shard_map/all_to_all | solution.py:138
  328.9 20.0 %subtract_subtract_fusion = (f32[1,16,128,1024]{3,2,1,0:T(8,128)}, f32[1,16,128,1024]{3,2,1,0:T(8,128)}) fusion(f32[2,16,128,1024]{3,2,1,0:T(8,128)} %get-tuple-element.23, f32[2,16,128,1024]{3,2,1,0:T(8,128)} %get-tuple-element.22, f32[128,1024]{1,0:T(8,128)S(1)} %copy-done.10, f32[128,1024]{1,0:T(8,128)S(1)} %copy.30, f32[128,1024]{1,0:T(8,128)S(1)} %copy.29), kind=kLoop, calls=%fused_computation.11 | loop fusion | flops 29360128 | bytes 51904512 | tf_op jit(solution)/shard_map/sub | solution.py:83
  348.9 17.2 %fusion.3 = f32[2,16,128,1024]{3,2,1,0:T(8,128)} fusion(f32[2,16,128,1024]{3,2,1,0:T(8,128)} %param.12, f32[1,16,128,1024]{3,2,1,0:T(8,128)} %get-tuple-element.5, f32[1,16,128,1024]{3,2,1,0:T(8,128)} %get-tuple-element.4), kind=kLoop, calls=%fused_computation.7 | loop fusion | flops 12582912 | bytes 50331648 | tf_op jit(solution)/shard_map/add | solution.py:105
  366.1 6.2 %fusion.31 = f32[2,128,1024]{2,1,0:T(8,128)S(1)} fusion(f32[1024,1024,1]{1,0,2:T(8,128)} %constant.31, f32[2,2,128,1024]{3,2,0,1:T(8,128)} %all-gather.5.cloned.1.call-done), kind=kOutput, calls=%fused_computation.88 | convolution fusion | flops 3221225472 | bytes 6291456 | tf_op jit(solution)/shard_map/fmn,nk->fmk/dot_general | solution.py:54
  372.3 6.2 %fusion.30 = f32[2,128,1024]{2,1,0:T(8,128)S(1)} fusion(f32[1024,1024,1]{1,0,2:T(8,128)} %constant.31, f32[2,2,128,1024]{3,2,0,1:T(8,128)} %all-gather.5.cloned.1.call-done), kind=kOutput, calls=%fused_computation.87 | convolution fusion | flops 3221225472 | bytes 6291456 | tf_op jit(solution)/shard_map/fmn,nk->fmk/dot_general | solution.py:54
  (78 shorter events, 37.7 us)
Async XLA Ops:
  7.2 212.6 %copy-start = (f32[16]{0:T(128)S(1)}, f32[16]{0:T(128)}, u32[]{:S(2)}) copy-start(f32[16]{0:T(128)} %param.14) | copy-start | bytes 196
  7.2 7.9 %copy-start.5 = (f32[2,128,1024]{2,1,0:T(8,128)S(1)}, f32[2,128,1024]{2,1,0:T(8,128)}, u32[]{:S(2)}) copy-start(f32[2,128,1024]{2,1,0:T(8,128)} %param.10) | copy-start | bytes 3145732
  7.2 7.9 %copy-start.6 = (f32[2,128,1024]{2,1,0:T(8,128)S(1)}, f32[2,128,1024]{2,1,0:T(8,128)}, u32[]{:S(2)}) copy-start(f32[2,128,1024]{2,1,0:T(8,128)} %param.9) | copy-start | bytes 3145732
  7.2 103.0 %all-gather.3.cloned.1.call-start = ((), (), s32[]{:S(2)}) async-start(), calls=%async_computation.5 | async-start | bytes 2621440 | tf_op jit(solution)/shard_map/all_gather | solution.py:150
  39.8 12.7 %copy-start.1 = (f32[1024,1024,1]{1,0,2:T(8,128)S(1)}, f32[1024,1024,1]{1,0,2:T(8,128)}, u32[]{:S(2)}) copy-start(f32[1024,1024,1]{1,0,2:T(8,128)} %constant.32) | copy-start | bytes 12582916
  69.8 42.8 %copy-start.9 = (f32[128,1024]{1,0:T(8,128)S(1)}, f32[128,1024]{1,0:T(8,128)}, u32[]{:S(2)}) copy-start(f32[128,1024]{1,0:T(8,128)} %param.15) | copy-start | bytes 1572868
  88.4 179.0 %reduce-scatter.2.cloned.1.call-start = ((), (), s32[]{:S(2)}) async-start(), calls=%async_computation.6 | async-start | bytes 1310720 | tf_op jit(solution)/shard_map/reduce_scatter | solution.py:166
  112.7 18.4 %copy-start.11 = (f32[16]{0:T(128)S(1)}, f32[16]{0:T(128)}, u32[]{:S(2)}) copy-start(f32[16]{0:T(128)} %param.13) | copy-start | bytes 196
  213.6 6.2 %copy-start.4 = (f32[2,16,128,1024]{3,2,1,0:T(8,128)}, f32[2,16,128,1024]{3,2,1,0:T(8,128)S(1)}, u32[]{:S(2)}) copy-start(f32[2,16,128,1024]{3,2,1,0:T(8,128)S(1)} %fusion.2) | copy-start | bytes 50331652
  219.7 22.7 %copy-start.7 = (f32[2,2,128,1024]{2,3,1,0:T(8,128)S(1)}, f32[2,2,128,1024]{2,3,1,0:T(8,128)}, u32[]{:S(2)}) copy-start(f32[2,2,128,1024]{2,3,1,0:T(8,128)} %all-gather.3.cloned.1.call-done) | copy-start | bytes 6291460
  242.3 123.8 %all-gather.5.cloned.1.call-start = ((), (), s32[]{:S(2)}) async-start(), calls=%async_computation.7 | async-start | bytes 2621440 | tf_op jit(solution)/shard_map/all_gather | solution.py:150
  289.0 12.7 %copy-start.2 = (f32[1024,1024,1]{1,0,2:T(8,128)S(1)}, f32[1024,1024,1]{1,0,2:T(8,128)}, u32[]{:S(2)}) copy-start(f32[1024,1024,1]{1,0,2:T(8,128)} %constant.32) | copy-start | bytes 12582916
  301.7 27.2 %copy-start.10 = (f32[128,1024]{1,0:T(8,128)S(1)}, f32[128,1024]{1,0:T(8,128)}, u32[]{:S(2)}) copy-start(f32[128,1024]{1,0:T(8,128)} %param.15) | copy-start | bytes 1572868
  366.1 12.4 %copy-start.3 = (f32[1024,1024,1]{1,0,2:T(8,128)S(1)}, f32[1024,1024,1]{1,0,2:T(8,128)}, u32[]{:S(2)}) copy-start(f32[1024,1024,1]{1,0,2:T(8,128)} %constant.32) | copy-start | bytes 12582916
  366.1 12.4 %copy-start.8 = (f32[2,2,128,1024]{3,2,0,1:T(8,128)S(1)}, f32[2,2,128,1024]{3,2,0,1:T(8,128)}, u32[]{:S(2)}) copy-start(f32[2,2,128,1024]{3,2,0,1:T(8,128)} %all-gather.5.cloned.1.call-done) | copy-start | bytes 6291460
Sparse Core Ops, SparseCore 0:
  88.5 21.6 all-gather.2
  242.5 24.8 reduce-scatter.1
  329.0 20.6 all-gather.4
